TPU v7x, 1024 devices: a whole 4x4x32 slice. The times are simulated.
1024 devices in a mesh: energy: 32 (over y, z_lo), momentum: 32 (over x, z_hi, core).
Axes of the slice: x: 4, y: 4, z: 32 (z_hi: 4, z_lo: 8; z = z_hi * 8 + z_lo), core: 2. Of those that a mesh axis runs over, the one named last changes fastest.
Arguments:
- device_hamiltonian: float32 [32, 2, 256, 256], P('momentum'), may hold values from -3 to 1, as said below
- lead_hamiltonian: float32 [32, 2, 256, 256], P('momentum'), may hold values from -3 to 1, as said below
- lead_coupling: float32 [32, 2, 256, 256], P('momentum'), may hold values from -0.28 to 0.28
- pair_atoms: int32 [2, 128], replicated, may hold values from 0 to 20, as said below
- phonon_shift: int32 [4], replicated, may hold values from 1 to 31
- occupation: float32 [4], replicated, may hold values from 0.2 to 1.5
- phonon_coupling: float32 [4, 128], replicated, may hold values from 0.1 to 0.4
Outputs:
- green_final: float32 [32, 32, 2, 256, 256], P('energy', 'momentum')
Inputs may be any that keep to these rules, and one draw needn't show every extreme that they name: `device_hamiltonian`: each diagonal entry has its real part in [-1, 1] and its imaginary part in [-3, -1.5]; off-diagonal entries lie within 0.21 in magnitude. `lead_hamiltonian`: each diagonal entry has its real part in [-1, 1] and its imaginary part in [-3, -1.5]; off-diagonal entries lie within 0.12 in magnitude. `pair_atoms`: the first 21 pairs join each atom with itself, in order; every other pair joins two different atoms.
All inputs are finite; a program needn't handle non-finite values.
Results may differ from a plain program's by a relative error of at most 0.00011.
Values sent between devices are 32-bit elements; how exact they have to be, the bound alone decides.
No kernel may reach another device: no remote copies, remote signals or barrier semaphores. Data moves between devices by JAX's collectives and lax.ppermute only.
A program may use at most 64 MiB of HBM per device.

v0:
```python
import jax
import jax.numpy as jnp
from jax import lax
from jax.experimental import pallas as pl
from jax.experimental.pallas import tpu as pltpu
from jax.sharding import Mesh
from jax.sharding import PartitionSpec as P

B = 256
ORB = 12
ATOMS = 21
PAIRS = 128
MODES = 4
MOMENTA = 32
ROWS = 2 * ORB * ORB
HALVES = (ATOMS + 1) // 2

INTERPRET = False


def split(value):
    high = value.astype(jnp.bfloat16)
    low = (value - high.astype(jnp.float32)).astype(jnp.bfloat16)
    return high, low


def split_complex(real, imag):
    real_high, real_low = split(real)
    imag_high, imag_low = split(imag)
    return real_high, real_low, imag_high, imag_low


def left_factors(parts):
    real_high, real_low, imag_high, imag_low = parts
    plain = [real_high, real_high, real_low]
    turned = [imag_high, imag_high, imag_low]
    minus = [-imag_high, -imag_high, -imag_low]
    return (
        jnp.concatenate(plain + minus, axis=1),
        jnp.concatenate(plain + turned, axis=1),
    )


def dot(left, right):
    return lax.dot_general(
        left, right, (((1,), (0,)), ((), ())), preferred_element_type=jnp.float32
    )


def dot_transposed(left, right):
    return lax.dot_general(
        left, right, (((1,), (1,)), ((), ())), preferred_element_type=jnp.float32
    )


def times(left, right_parts, transposed=False):
    for_real, for_imag = left
    real_high, real_low, imag_high, imag_low = right_parts
    axis = 1 if transposed else 0
    product = dot_transposed if transposed else dot
    real_right = jnp.concatenate(
        [real_high, real_low, real_high, imag_high, imag_low, imag_high], axis=axis
    )
    imag_right = jnp.concatenate(
        [imag_high, imag_low, imag_high, real_high, real_low, real_high], axis=axis
    )
    return product(for_real, real_right), product(for_imag, imag_right)


def add(left, right):
    return left[0] + right[0], left[1] + right[1]


def grid_of(axis, shape=(B, B)):
    return lax.broadcasted_iota(jnp.int32, shape, axis)


def inverse_of(system, bare):
    system_real, system_imag = system
    bare_real, bare_imag = bare
    identity = (grid_of(0) == grid_of(1)).astype(jnp.float32)
    diag_real = jnp.sum(bare_real * identity, axis=0, keepdims=True)
    diag_imag = jnp.sum(bare_imag * identity, axis=0, keepdims=True)
    modulus = diag_real * diag_real + diag_imag * diag_imag
    row_real = diag_real / modulus
    row_imag = -diag_imag / modulus
    column_real = jnp.sum(identity * row_real, axis=1, keepdims=True)
    column_imag = jnp.sum(identity * row_imag, axis=1, keepdims=True)
    error_real = identity - (column_real * system_real - column_imag * system_imag)
    error_imag = -(column_real * system_imag + column_imag * system_real)
    plus_real = identity + error_real
    start = (
        plus_real * row_real - error_imag * row_imag,
        plus_real * row_imag + error_imag * row_real,
    )
    error_parts = split_complex(error_real, error_imag)
    squared = times(left_factors(error_parts), error_parts)
    return two_more(squared, start)


def two_more(squared, start):
    squared_parts = split_complex(*squared)
    squared_left = left_factors(squared_parts)
    first = add(start, times(squared_left, split_complex(*start)))
    fourth = times(squared_left, squared_parts)
    fourth_left = left_factors(split_complex(*fourth))
    return add(first, times(fourth_left, split_complex(*first)))


def first_kernel(
    energy_ref, device_ref, lead_ref, coupling_ref, pair_ref, system_ref, green_ref, blocks_ref, rows_ref
):
    energy = energy_ref[0]
    scaled_identity = jnp.where(grid_of(0) == grid_of(1), energy, 0.0)
    lead = (scaled_identity - lead_ref[0, 0], -lead_ref[0, 1])
    green_lead = inverse_of(lead, lead)
    coupling_parts = split_complex(coupling_ref[0, 0], coupling_ref[0, 1])
    half = times(left_factors(coupling_parts), split_complex(*green_lead))
    contact = times(left_factors(split_complex(*half)), coupling_parts, transposed=True)
    bare = (scaled_identity - device_ref[0, 0], -device_ref[0, 1])
    system = (bare[0] - contact[0], bare[1] - contact[1])
    system_ref[0] = system[0]
    system_ref[1] = system[1]
    green = inverse_of(system, bare)
    green_ref[0] = green[0]
    green_ref[1] = green[1]
    take_blocks(green, pair_ref, rows_ref)
    shards, shard_rows = blocks_ref.shape[:2]
    for shard in range(shards):
        blocks_ref[shard] = rows_ref[shard * shard_rows : (shard + 1) * shard_rows, :]


def take_blocks(green, pair_ref, rows_ref):
    real_high, real_low = split(green[0])
    imag_high, imag_low = split(green[1])
    left = jnp.concatenate(
        [
            jnp.concatenate([real_high, real_low], axis=1),
            jnp.concatenate([imag_high, imag_low], axis=1),
        ],
        axis=0,
    )
    row_atom = pair_ref[0:1, :]
    column_atom = pair_ref[1:2, :]
    row_half = row_atom // 2
    row_odd = (row_atom - 2 * row_half) == 1
    row_half = jnp.concatenate([row_half, row_half], axis=1)
    row_odd = jnp.concatenate([row_atom, row_atom], axis=1) - 2 * row_half == 1
    offset = grid_of(0, (B, PAIRS)) - ORB * column_atom
    for first in range(0, ORB, 2):
        pick = jnp.concatenate(
            [(offset == first).astype(jnp.bfloat16), (offset == first + 1).astype(jnp.bfloat16)],
            axis=1,
        )
        columns = dot(left, jnp.concatenate([pick, pick], axis=0))
        for part in range(2):
            found = jnp.zeros((2 * ORB, 2 * PAIRS), jnp.float32)
            for half in range(HALVES):
                begin = part * B + 2 * ORB * half
                if half == HALVES - 1:
                    piece = jnp.concatenate(
                        [columns[begin : begin + 16], jnp.zeros((8, 2 * PAIRS), jnp.float32)], axis=0
                    )
                else:
                    piece = columns[begin : begin + 2 * ORB]
                found = jnp.where(row_half == half, piece, found)
            chosen = jnp.where(row_odd, found[ORB:], found[:ORB])
            for side in range(2):
                row = (part * ORB + first + side) * ORB
                rows_ref[row : row + ORB, :] = chosen[:, side * PAIRS : (side + 1) * PAIRS]


def place_blocks(values, pair_ref):
    row_atom = pair_ref[0:1, :]
    column_atom = pair_ref[1:2, :]
    row_half = row_atom // 2
    row_odd = row_atom - 2 * row_half
    identity = grid_of(0, (PAIRS, PAIRS)) == grid_of(1, (PAIRS, PAIRS))
    column_of = jnp.sum(
        jnp.where(identity, (ORB * column_atom).astype(jnp.float32), 0.0), axis=1, keepdims=True
    ).astype(jnp.int32)
    offset = grid_of(1, (PAIRS, B)) - column_of
    pick = jnp.concatenate(
        [(offset == column).astype(jnp.bfloat16) for column in range(ORB)], axis=0
    )
    results = []
    for part in range(2):
        highs = []
        lows = []
        for column in range(ORB):
            row = (part * ORB + column) * ORB
            block = values[row : row + ORB, :]
            both = jnp.concatenate(
                [jnp.where(row_odd == 0, block, 0.0), jnp.where(row_odd == 1, block, 0.0)], axis=0
            )
            pieces = []
            for half in range(HALVES):
                piece = jnp.where(row_half == half, both, 0.0)
                pieces.append(piece[:16] if half == HALVES - 1 else piece)
            spread = jnp.concatenate(pieces, axis=0)
            high, low = split(spread)
            highs.append(high)
            lows.append(low)
        left = jnp.concatenate(highs + lows, axis=1)
        results.append(dot(left, jnp.concatenate([pick, pick], axis=0)))
    return results


def last_kernel(system_ref, green_ref, blocks_ref, pair_ref, out_ref):
    shards, shard_rows = blocks_ref.shape[:2]
    values = jnp.concatenate([blocks_ref[shard] for shard in range(shards)], axis=0)
    scattering = place_blocks(values, pair_ref)
    second = (system_ref[0] - scattering[0], system_ref[1] - scattering[1])
    green = (green_ref[0], green_ref[1])
    identity = (grid_of(0) == grid_of(1)).astype(jnp.float32)
    product = times(left_factors(split_complex(*green)), split_complex(*second))
    residual = (identity - product[0], -product[1])
    final = two_more(residual, green)
    out_ref[0, 0, 0] = final[0]
    out_ref[0, 0, 1] = final[1]


def vmem(count):
    return [pl.BlockSpec(memory_space=pltpu.VMEM)] * count


def first_call(energy, device_hamiltonian, lead_hamiltonian, lead_coupling, pair_atoms, shards):
    shape = jax.ShapeDtypeStruct((2, B, B), jnp.float32)
    blocks = jax.ShapeDtypeStruct((shards, ROWS // shards, PAIRS), jnp.float32)
    return pl.pallas_call(
        first_kernel,
        out_shape=(shape, shape, blocks),
        in_specs=[pl.BlockSpec(memory_space=pltpu.SMEM)] + vmem(4),
        out_specs=tuple(vmem(3)),
        scratch_shapes=[pltpu.VMEM((ROWS, PAIRS), jnp.float32)],
        name="first_round",
        interpret=INTERPRET,
    )(energy, device_hamiltonian, lead_hamiltonian, lead_coupling, pair_atoms)


def last_call(system, green, blocks, pair_atoms):
    return pl.pallas_call(
        last_kernel,
        out_shape=jax.ShapeDtypeStruct((1, 1, 2, B, B), jnp.float32),
        in_specs=vmem(4),
        out_specs=pl.BlockSpec(memory_space=pltpu.VMEM),
        name="second_round",
        interpret=INTERPRET,
    )(system, green, blocks, pair_atoms)


def exchange(array, axes):
    return lax.all_to_all(array, axes, split_axis=0, concat_axis=0, tiled=True)


def slab_sum_kernel(arrived_ref, out_ref, sums_ref):
    groups, rows = sums_ref.shape[0] // arrived_ref.shape[1], arrived_ref.shape[1]
    members = arrived_ref.shape[0] // groups
    for group in range(groups):
        total = arrived_ref[group * members]
        for member in range(1, members):
            total = total + arrived_ref[group * members + member]
        sums_ref[group * rows : (group + 1) * rows, :] = total
    for copy in range(out_ref.shape[0]):
        out_ref[copy] = sums_ref[...]


def column_sum_kernel(arrived_ref, out_ref):
    total = arrived_ref[0]
    for member in range(1, arrived_ref.shape[0]):
        total = total + arrived_ref[member]
    for copy in range(out_ref.shape[0]):
        out_ref[copy] = total


def convolve_kernel(lane_ref, shift_ref, occupation_ref, coupling_ref, arrived_ref, out_ref):
    lanes, stacked = arrived_ref.shape[:2]
    rows = out_ref.shape[1]
    planes = stacked // rows
    copies = out_ref.shape[0] // planes
    energies = lanes * planes
    source = lax.broadcasted_iota(jnp.int32, (energies, PAIRS), 0)
    weights = []
    for plane in range(planes):
        target = plane * lanes + lane_ref[0]
        total = jnp.zeros((energies, PAIRS), jnp.float32)
        for mode in range(MODES):
            occupied = occupation_ref[mode]
            shift = shift_ref[mode]
            factor = jnp.where(source == target - shift, occupied, 0.0) + jnp.where(
                source == target + shift, occupied + 1.0, 0.0
            )
            total = total + factor * coupling_ref[mode : mode + 1, :]
        weights.append(total / MOMENTA)
    results = [jnp.zeros((rows, PAIRS), jnp.float32) for _ in range(planes)]
    for lane in range(lanes):
        for plane in range(planes):
            piece = arrived_ref[lane, plane * rows : (plane + 1) * rows, :]
            energy = plane * lanes + lane
            for target in range(planes):
                results[target] = results[target] + weights[target][energy : energy + 1, :] * piece
    for plane in range(planes):
        for copy in range(copies):
            out_ref[plane * copies + copy] = results[plane]


def per_device(
    device_hamiltonian,
    lead_hamiltonian,
    lead_coupling,
    pair_atoms,
    phonon_shift,
    occupation,
    phonon_coupling,
):
    planes = lax.axis_size("y")
    lanes = lax.axis_size("z_lo")
    columns = lax.axis_size("z_hi")
    slab = planes * lax.axis_size("x") * lax.axis_size("core")
    rows = ROWS // slab
    energy_index = lax.axis_index(("y", "z_lo"))
    energy = -1.0 + 2.0 * (energy_index.astype(jnp.float32) + 0.5) / (planes * lanes)
    system, green, blocks = first_call(
        energy[None], device_hamiltonian, lead_hamiltonian, lead_coupling, pair_atoms, slab
    )
    arrived = exchange(blocks, ("y", "x", "core"))
    summed = pl.pallas_call(
        slab_sum_kernel,
        out_shape=jax.ShapeDtypeStruct((columns, planes * rows, PAIRS), jnp.float32),
        in_specs=vmem(1),
        out_specs=vmem(1)[0],
        scratch_shapes=[pltpu.VMEM((planes * rows, PAIRS), jnp.float32)],
        name="slab_sum",
        interpret=INTERPRET,
    )(arrived)
    arrived = exchange(summed, "z_hi")
    summed = pl.pallas_call(
        column_sum_kernel,
        out_shape=jax.ShapeDtypeStruct((lanes, planes * rows, PAIRS), jnp.float32),
        in_specs=vmem(1),
        out_specs=vmem(1)[0],
        name="column_sum",
        interpret=INTERPRET,
    )(arrived)
    arrived = exchange(summed, "z_lo")
    self_energy = pl.pallas_call(
        convolve_kernel,
        out_shape=jax.ShapeDtypeStruct((slab, rows, PAIRS), jnp.float32),
        in_specs=[pl.BlockSpec(memory_space=pltpu.SMEM)] * 3 + vmem(2),
        out_specs=vmem(1)[0],
        name="phonon_sum",
        interpret=INTERPRET,
    )(lax.axis_index("z_lo")[None], phonon_shift, occupation, phonon_coupling, arrived)
    arrived = exchange(self_energy, ("y", "x", "core"))
    return last_call(system, green, arrived, pair_atoms)


def solution(mesh):
    momentum = ("x", "z_hi", "core")
    split_mesh = Mesh(mesh.devices.reshape(4, 8, 4, 4, 2), ("y", "z_lo") + momentum)
    return jax.shard_map(
        per_device,
        mesh=split_mesh,
        in_specs=(P(momentum),) * 3 + (P(),) * 4,
        out_specs=P(("y", "z_lo"), momentum),
        check_vma=False,
    )
```

profile of v0, /device:TPU:1, one launch (start us, length us, event | category | flops | bytes accessed | tf_op | source)
XLA Modules:
  0.0 121.7 jit_solution(301175444401127513)
XLA Ops:
  0.0 8.3 %first_round.1 = (f32[2,256,256]{2,1,0:T(8,128)}, f32[2,256,256]{2,1,0:T(8,128)}, f32[32,9,128]{2,1,0:T(8,128)}) custom-call(f32[1]{0:T(128)} %bitcast.energy_ref, f32[1,2,256,256]{3,2,1,0:T(8,128)} %device_ref.1, f32[1,2,256,256]{3,2,1,0:T(8,128)} %lead_ref.1, f32[1,2,256,256]{3,2,1,0:T(8,128)} %coupling_ref.2, s32[2,128]{1,0:T(2,128)} %pair_ref.3), custom_call_target="tpu_custom_call" | custom-call | tf_op jit(solution)/shard_map/first_round/pallas_call | solution.py:230
  8.3 27.3 %all_to_all.20.arrived_ref = f32[32,9,128]{2,1,0:T(8,128)} all-to-all(f32[32,9,128]{2,1,0:T(8,128)} %get-tuple-element.10), channel_id=1, replica_groups=mesh['y'=4,'z_lo'=8,'x'=4,'z_hi'=4,'core'=2] {'y','x','core'}, dimensions={0} | all-to-all | bytes 294912 | tf_op jit(solution)/shard_map/all_to_all | solution.py:253
  35.6 1.6 %slab_sum.1 = f32[4,36,128]{2,1,0:T(8,128)} custom-call(f32[32,9,128]{2,1,0:T(8,128)} %all_to_all.20.arrived_ref), custom_call_target="tpu_custom_call" | custom-call | tf_op jit(solution)/shard_map/slab_sum/pallas_call | solution.py:327
  37.2 40.1 %all_to_all.21.arrived_ref = f32[4,36,128]{2,1,0:T(8,128)} all-to-all(f32[4,36,128]{2,1,0:T(8,128)} %slab_sum.1), channel_id=1, replica_groups=mesh['y'=4,'z_lo'=8,'x'=4,'z_hi'=4,'core'=2] {'z_hi'}, dimensions={0} | all-to-all | bytes 147456 | tf_op jit(solution)/shard_map/all_to_all | solution.py:253
  77.2 1.6 %column_sum.1 = f32[8,36,128]{2,1,0:T(8,128)} custom-call(f32[4,36,128]{2,1,0:T(8,128)} %all_to_all.21.arrived_ref), custom_call_target="tpu_custom_call" | custom-call | tf_op jit(solution)/shard_map/column_sum/pallas_call | solution.py:337
  78.8 15.5 %all_to_all.22.arrived_ref = f32[8,36,128]{2,1,0:T(8,128)} all-to-all(f32[8,36,128]{2,1,0:T(8,128)} %column_sum.1), channel_id=1, replica_groups=mesh['y'=4,'z_lo'=8,'x'=4,'z_hi'=4,'core'=2] {'z_lo'}, dimensions={0} | all-to-all | bytes 294912 | tf_op jit(solution)/shard_map/all_to_all | solution.py:253
  94.3 1.8 %phonon_sum.1 = f32[32,9,128]{2,1,0:T(8,128)} custom-call(s32[1]{0:T(128)} %bitcast.1.lane_ref, s32[4]{0:T(128)} %shift_ref.1, f32[4]{0:T(128)} %occupation_ref.1, f32[4,128]{1,0:T(4,128)} %coupling_ref.3, f32[8,36,128]{2,1,0:T(8,128)} %all_to_all.22.arrived_ref), custom_call_target="tpu_custom_call" | custom-call | tf_op jit(solution)/shard_map/phonon_sum/pallas_call | solution.py:346
  96.1 20.5 %all_to_all.23.blocks_ref = f32[32,9,128]{2,1,0:T(8,128)} all-to-all(f32[32,9,128]{2,1,0:T(8,128)} %phonon_sum.1), channel_id=1, replica_groups=mesh['y'=4,'z_lo'=8,'x'=4,'z_hi'=4,'core'=2] {'y','x','core'}, dimensions={0} | all-to-all | bytes 294912 | tf_op jit(solution)/shard_map/all_to_all | solution.py:253
  116.6 5.1 %second_round.1 = f32[1,1,2,256,256]{4,3,2,1,0:T(8,128)} custom-call(f32[2,256,256]{2,1,0:T(8,128)} %get-tuple-element.8.system_ref, f32[2,256,256]{2,1,0:T(8,128)} %get-tuple-element.9.green_ref, f32[32,9,128]{2,1,0:T(8,128)} %all_to_all.23.blocks_ref, s32[2,128]{1,0:T(2,128)} %pair_ref.3), custom_call_target="tpu_custom_call" | custom-call | tf_op jit(solution)/shard_map/second_round/pallas_call | solution.py:242
where the time goes:
time: 122 us
  blocking collectives  103 us (84%)
  Pallas kernels  18.4 us (15%)
    all_to_all x4, blocking collectives, exchange(): return lax.all_to_all(array, axes, split_axis=0, concat_axis=0, tiled=True)  103 us
    pallas_call x1, Pallas kernels, first_call(): pl.pallas_call(first_kernel, out_shape=(shape, shape, blocks), in_specs=[...  8.26 us
    pallas_call x1, Pallas kernels, last_call(): pl.pallas_call(last_kernel, out_shape=jax.ShapeDtypeStruct((1, 1, 2, B, B...  5.09 us

commit v1 on v0

--- a/solution.py
+++ b/solution.py
@@ -253,24 +253,15 @@
     return lax.all_to_all(array, axes, split_axis=0, concat_axis=0, tiled=True)
 
 
-def slab_sum_kernel(arrived_ref, out_ref, sums_ref):
-    groups, rows = sums_ref.shape[0] // arrived_ref.shape[1], arrived_ref.shape[1]
+def slab_sum_kernel(arrived_ref, out_ref):
+    rows = arrived_ref.shape[1]
+    groups = out_ref.shape[0] // rows
     members = arrived_ref.shape[0] // groups
     for group in range(groups):
         total = arrived_ref[group * members]
         for member in range(1, members):
             total = total + arrived_ref[group * members + member]
-        sums_ref[group * rows : (group + 1) * rows, :] = total
-    for copy in range(out_ref.shape[0]):
-        out_ref[copy] = sums_ref[...]
-
-
-def column_sum_kernel(arrived_ref, out_ref):
-    total = arrived_ref[0]
-    for member in range(1, arrived_ref.shape[0]):
-        total = total + arrived_ref[member]
-    for copy in range(out_ref.shape[0]):
-        out_ref[copy] = total
+        out_ref[group * rows : (group + 1) * rows, :] = total
 
 
 def convolve_kernel(lane_ref, shift_ref, occupation_ref, coupling_ref, arrived_ref, out_ref):
@@ -315,7 +306,6 @@
 ):
     planes = lax.axis_size("y")
     lanes = lax.axis_size("z_lo")
-    columns = lax.axis_size("z_hi")
     slab = planes * lax.axis_size("x") * lax.axis_size("core")
     rows = ROWS // slab
     energy_index = lax.axis_index(("y", "z_lo"))
@@ -326,23 +316,17 @@
     arrived = exchange(blocks, ("y", "x", "core"))
     summed = pl.pallas_call(
         slab_sum_kernel,
-        out_shape=jax.ShapeDtypeStruct((columns, planes * rows, PAIRS), jnp.float32),
+        out_shape=jax.ShapeDtypeStruct((planes * rows, PAIRS), jnp.float32),
         in_specs=vmem(1),
         out_specs=vmem(1)[0],
-        scratch_shapes=[pltpu.VMEM((planes * rows, PAIRS), jnp.float32)],
         name="slab_sum",
         interpret=INTERPRET,
     )(arrived)
-    arrived = exchange(summed, "z_hi")
-    summed = pl.pallas_call(
-        column_sum_kernel,
-        out_shape=jax.ShapeDtypeStruct((lanes, planes * rows, PAIRS), jnp.float32),
-        in_specs=vmem(1),
-        out_specs=vmem(1)[0],
-        name="column_sum",
-        interpret=INTERPRET,
-    )(arrived)
-    arrived = exchange(summed, "z_lo")
+    near = lax.ppermute(summed, "z_hi", [(0, 1), (1, 0), (2, 3), (3, 2)])
+    paired = summed + near
+    far = lax.ppermute(paired, "z_hi", [(0, 3), (3, 0), (1, 2), (2, 1)])
+    copies = jnp.broadcast_to(paired + far, (lanes, planes * rows, PAIRS))
+    arrived = exchange(copies, "z_lo")
     self_energy = pl.pallas_call(
         convolve_kernel,
         out_shape=jax.ShapeDtypeStruct((slab, rows, PAIRS), jnp.float32),

time: 122 us -> 105 us (0.86)
  blocking collectives: 103 us -> 59.6 us
  starting transfers between devices: 0 us -> 18.6 us
  waiting for transfers between devices: 0 us -> 8.92 us
  Pallas kernels: 18.4 us -> 16.8 us
    all_to_all x4 -> x3, blocking collectives: 103 us -> 59.6 us  [exchange(): return lax.all_to_all(array, axes, split_axis=0, concat_axis=0, tiled=True)]
    ppermute x0 -> x2, starting transfers between devices: none -> 18.6 us  [the longest x1 12.9 us: per_device(): far = lax.ppermute(paired, 'z_hi', [(0, 3), (3, 0), (1, 2), (2, 1)])]
    ppermute x0 -> x2, waiting for transfers between devices: none -> 8.92 us  [the longest x1 7.76 us: per_device(): near = lax.ppermute(summed, 'z_hi', [(0, 1), (1, 0), (2, 3), (3, 2)])]
    pallas_call x2 -> x1, Pallas kernels: 3.18 us -> 1.57 us  [per_device(): pl.pallas_call(slab_sum_kernel, out_shape=jax.ShapeDtypeStruct((planes *...]
  transfers between devices with their start and end apart: 0 -> 2, of which waited for: 0 -> 2; matrix products, arithmetic and copies ran while one was open for 0% -> 0% of each run, Pallas kernels for 0% -> 0%
where the time goes in v1:
time: 105 us
  blocking collectives  59.6 us (57%)
  starting transfers between devices  18.6 us (18%)
  Pallas kernels  16.8 us (16%)
  waiting for transfers between devices  8.92 us (8%)
    all_to_all x3, blocking collectives, exchange(): return lax.all_to_all(array, axes, split_axis=0, concat_axis=0, tiled=True)  59.6 us
    ppermute x1, starting transfers between devices, per_device(): far = lax.ppermute(paired, 'z_hi', [(0, 3), (3, 0), (1, 2), (2, 1)])  12.9 us
    pallas_call x1, Pallas kernels, first_call(): pl.pallas_call(first_kernel, out_shape=(shape, shape, blocks), in_specs=[...  8.26 us
    ppermute x1, waiting for transfers between devices, per_device(): near = lax.ppermute(summed, 'z_hi', [(0, 1), (1, 0), (2, 3), (3, 2)])  7.76 us
    ppermute x1, starting transfers between devices, per_device(): near = lax.ppermute(summed, 'z_hi', [(0, 1), (1, 0), (2, 3), (3, 2)])  5.67 us
    pallas_call x1, Pallas kernels, last_call(): pl.pallas_call(last_kernel, out_shape=jax.ShapeDtypeStruct((1, 1, 2, B, B...  5.09 us
  transfers between devices with their start and end apart: 2, of which 2 were waited for; matrix products, arithmetic and copies ran while one was open for 0% of the time, Pallas kernels for 0%

profile of v1, /device:TPU:1, one launch (start us, length us, event | category | flops | bytes accessed | tf_op | source)
XLA Modules:
  0.0 104.7 jit_solution(15941594135093752231)
XLA Ops:
  0.0 8.3 %first_round.1 = (f32[2,256,256]{2,1,0:T(8,128)}, f32[2,256,256]{2,1,0:T(8,128)}, f32[32,9,128]{2,1,0:T(8,128)}) custom-call(f32[1]{0:T(128)} %bitcast.energy_ref, f32[1,2,256,256]{3,2,1,0:T(8,128)} %device_ref.1, f32[1,2,256,256]{3,2,1,0:T(8,128)} %lead_ref.1, f32[1,2,256,256]{3,2,1,0:T(8,128)} %coupling_ref.2, s32[2,128]{1,0:T(2,128)} %pair_ref.3), custom_call_target="tpu_custom_call" | custom-call | tf_op jit(solution)/shard_map/first_round/pallas_call | solution.py:230
  8.3 27.3 %all_to_all.15.arrived_ref = f32[32,9,128]{2,1,0:T(8,128)} all-to-all(f32[32,9,128]{2,1,0:T(8,128)} %get-tuple-element.10), channel_id=1, replica_groups=mesh['y'=4,'z_lo'=8,'x'=4,'z_hi'=4,'core'=2] {'y','x','core'}, dimensions={0} | all-to-all | bytes 294912 | tf_op jit(solution)/shard_map/all_to_all | solution.py:253
  35.6 1.6 %slab_sum.1 = f32[36,128]{1,0:T(8,128)} custom-call(f32[32,9,128]{2,1,0:T(8,128)} %all_to_all.15.arrived_ref), custom_call_target="tpu_custom_call" | custom-call | tf_op jit(solution)/shard_map/slab_sum/pallas_call | solution.py:317
  37.1 5.7 %collective-permute-start = (f32[36,128]{1,0:T(8,128)}, f32[36,128]{1,0:T(8,128)S(1)}, u32[]{:S(2)}, u32[]{:S(2)}) collective-permute-start(f32[36,128]{1,0:T(8,128)} %slab_sum.1), channel_id=1, source_target_pairs={{0,2},{2,0},{4,6},{6,4},{1,3},{3,1},{5,7},{7,5},{8,10},{10,8},{12,... | collective-permute-start | bytes 55304 | tf_op jit(solution)/shard_map/ppermute | solution.py:325
  42.8 7.8 %collective-permute-done = f32[36,128]{1,0:T(8,128)S(1)} collective-permute-done((f32[36,128]{1,0:T(8,128)}, f32[36,128]{1,0:T(8,128)S(1)}, u32[]{:S(2)}, u32[]{:S(2)}) %collective-permute-start) | collective-permute-done | bytes 18464 | tf_op jit(solution)/shard_map/ppermute | solution.py:325
  50.6 0.7 add.14
  51.3 12.9 %collective-permute-start.1 = (f32[36,128]{1,0:T(8,128)S(1)}, f32[36,128]{1,0:T(8,128)S(1)}, u32[]{:S(2)}, u32[]{:S(2)}) collective-permute-start(f32[36,128]{1,0:T(8,128)S(1)} %add.14), channel_id=1, source_target_pairs={{0,6},{6,0},{2,4},{4,2},{1,7},{7,1},{3,5},{5,3},{8,14},{14,8},{10,... | collective-permute-start | bytes 55304 | tf_op jit(solution)/shard_map/ppermute | solution.py:327
  64.3 1.2 %collective-permute-done.1 = f32[36,128]{1,0:T(8,128)S(1)} collective-permute-done((f32[36,128]{1,0:T(8,128)S(1)}, f32[36,128]{1,0:T(8,128)S(1)}, u32[]{:S(2)}, u32[]{:S(2)}) %collective-permute-start.1) | collective-permute-done | bytes 18464 | tf_op jit(solution)/shard_map/ppermute | solution.py:327
  65.4 15.6 %all_to_all.16.arrived_ref = f32[8,36,128]{2,1,0:T(8,128)} all-to-all(f32[8,36,128]{2,1,0:T(8,128)S(1)} %broadcast_in_dim.11), channel_id=1, replica_groups=mesh['y'=4,'z_lo'=8,'x'=4,'z_hi'=4,'core'=2] {'z_lo'}, dimensions={0} | all-to-all | bytes 294912 | tf_op jit(solution)/shard_map/all_to_all | solution.py:253
  81.0 1.8 %phonon_sum.1 = f32[32,9,128]{2,1,0:T(8,128)} custom-call(s32[1]{0:T(128)} %bitcast.1.lane_ref, s32[4]{0:T(128)} %shift_ref.1, f32[4]{0:T(128)} %occupation_ref.1, f32[4,128]{1,0:T(4,128)} %coupling_ref.3, f32[8,36,128]{2,1,0:T(8,128)} %all_to_all.16.arrived_ref), custom_call_target="tpu_custom_call" | custom-call | tf_op jit(solution)/shard_map/phonon_sum/pallas_call | solution.py:330
  82.8 16.7 %all_to_all.17.blocks_ref = f32[32,9,128]{2,1,0:T(8,128)} all-to-all(f32[32,9,128]{2,1,0:T(8,128)} %phonon_sum.1), channel_id=1, replica_groups=mesh['y'=4,'z_lo'=8,'x'=4,'z_hi'=4,'core'=2] {'y','x','core'}, dimensions={0} | all-to-all | bytes 294912 | tf_op jit(solution)/shard_map/all_to_all | solution.py:253
  99.6 5.1 %second_round.1 = f32[1,1,2,256,256]{4,3,2,1,0:T(8,128)} custom-call(f32[2,256,256]{2,1,0:T(8,128)} %get-tuple-element.8.system_ref, f32[2,256,256]{2,1,0:T(8,128)} %get-tuple-element.9.green_ref, f32[32,9,128]{2,1,0:T(8,128)} %all_to_all.17.blocks_ref, s32[2,128]{1,0:T(2,128)} %pair_ref.3), custom_call_target="tpu_custom_call" | custom-call | tf_op jit(solution)/shard_map/second_round/pallas_call | solution.py:242
  (2 shorter events, 0.0 us)
Async XLA Ops:
  37.1 13.4 %collective-permute-start = (f32[36,128]{1,0:T(8,128)}, f32[36,128]{1,0:T(8,128)S(1)}, u32[]{:S(2)}, u32[]{:S(2)}) collective-permute-start(f32[36,128]{1,0:T(8,128)} %slab_sum.1), channel_id=1, source_target_pairs={{0,2},{2,0},{4,6},{6,4},{1,3},{3,1},{5,7},{7,5},{8,10},{10,8},{12,... | collective-permute-start | bytes 55304 | tf_op jit(solution)/shard_map/ppermute | solution.py:325
  51.3 14.1 %collective-permute-start.1 = (f32[36,128]{1,0:T(8,128)S(1)}, f32[36,128]{1,0:T(8,128)S(1)}, u32[]{:S(2)}, u32[]{:S(2)}) collective-permute-start(f32[36,128]{1,0:T(8,128)S(1)} %add.14), channel_id=1, source_target_pairs={{0,6},{6,0},{2,4},{4,2},{1,7},{7,1},{3,5},{5,3},{8,14},{14,8},{10,... | collective-permute-start | bytes 55304 | tf_op jit(solution)/shard_map/ppermute | solution.py:327

commit v2 on v1

--- a/solution.py
+++ b/solution.py
@@ -12,6 +12,9 @@
 PAIRS = 128
 MODES = 4
 MOMENTA = 32
+PLANES = 4
+LANES = 8
+SHARE = PAIRS // LANES
 ROWS = 2 * ORB * ORB
 HALVES = (ATOMS + 1) // 2
 
@@ -125,9 +128,11 @@
     green_ref[0] = green[0]
     green_ref[1] = green[1]
     take_blocks(green, pair_ref, rows_ref)
-    shards, shard_rows = blocks_ref.shape[:2]
-    for shard in range(shards):
-        blocks_ref[shard] = rows_ref[shard * shard_rows : (shard + 1) * shard_rows, :]
+    shards = blocks_ref.shape[0]
+    shard_rows = ROWS // shards
+    for row in range(ROWS):
+        place = (row % shard_rows) * PAIRS
+        blocks_ref[row // shard_rows, :, place : place + PAIRS] = rows_ref[row : row + 1, :]
 
 
 def take_blocks(green, pair_ref, rows_ref):
@@ -206,10 +211,12 @@
     return results
 
 
-def last_kernel(system_ref, green_ref, blocks_ref, pair_ref, out_ref):
-    shards, shard_rows = blocks_ref.shape[:2]
-    values = jnp.concatenate([blocks_ref[shard] for shard in range(shards)], axis=0)
-    scattering = place_blocks(values, pair_ref)
+def last_kernel(system_ref, green_ref, blocks_ref, pair_ref, out_ref, rows_ref):
+    shard_rows = ROWS // blocks_ref.shape[0]
+    for row in range(ROWS):
+        place = (row % shard_rows) * PAIRS
+        rows_ref[row : row + 1, :] = blocks_ref[row // shard_rows, :, place : place + PAIRS]
+    scattering = place_blocks(rows_ref, pair_ref)
     second = (system_ref[0] - scattering[0], system_ref[1] - scattering[1])
     green = (green_ref[0], green_ref[1])
     identity = (grid_of(0) == grid_of(1)).astype(jnp.float32)
@@ -226,7 +233,7 @@
 
 def first_call(energy, device_hamiltonian, lead_hamiltonian, lead_coupling, pair_atoms, shards):
     shape = jax.ShapeDtypeStruct((2, B, B), jnp.float32)
-    blocks = jax.ShapeDtypeStruct((shards, ROWS // shards, PAIRS), jnp.float32)
+    blocks = jax.ShapeDtypeStruct((shards, 1, ROWS // shards * PAIRS), jnp.float32)
     return pl.pallas_call(
         first_kernel,
         out_shape=(shape, shape, blocks),
@@ -244,6 +251,7 @@
         out_shape=jax.ShapeDtypeStruct((1, 1, 2, B, B), jnp.float32),
         in_specs=vmem(4),
         out_specs=pl.BlockSpec(memory_space=pltpu.VMEM),
+        scratch_shapes=[pltpu.VMEM((ROWS, PAIRS), jnp.float32)],
         name="second_round",
         interpret=INTERPRET,
     )(system, green, blocks, pair_atoms)
@@ -253,46 +261,114 @@
     return lax.all_to_all(array, axes, split_axis=0, concat_axis=0, tiled=True)
 
 
+def lanes_of(width=PAIRS):
+    return lax.broadcasted_iota(jnp.int32, (1, width), 1)
+
+
 def slab_sum_kernel(arrived_ref, out_ref):
-    rows = arrived_ref.shape[1]
-    groups = out_ref.shape[0] // rows
-    members = arrived_ref.shape[0] // groups
-    for group in range(groups):
-        total = arrived_ref[group * members]
+    members = arrived_ref.shape[0] // PLANES
+    totals = []
+    for plane in range(PLANES):
+        total = arrived_ref[plane * members]
         for member in range(1, members):
-            total = total + arrived_ref[group * members + member]
-        out_ref[group * rows : (group + 1) * rows, :] = total
-
-
-def convolve_kernel(lane_ref, shift_ref, occupation_ref, coupling_ref, arrived_ref, out_ref):
-    lanes, stacked = arrived_ref.shape[:2]
-    rows = out_ref.shape[1]
-    planes = stacked // rows
-    copies = out_ref.shape[0] // planes
-    energies = lanes * planes
-    source = lax.broadcasted_iota(jnp.int32, (energies, PAIRS), 0)
-    weights = []
-    for plane in range(planes):
-        target = plane * lanes + lane_ref[0]
-        total = jnp.zeros((energies, PAIRS), jnp.float32)
-        for mode in range(MODES):
-            occupied = occupation_ref[mode]
-            shift = shift_ref[mode]
-            factor = jnp.where(source == target - shift, occupied, 0.0) + jnp.where(
-                source == target + shift, occupied + 1.0, 0.0
-            )
-            total = total + factor * coupling_ref[mode : mode + 1, :]
-        weights.append(total / MOMENTA)
-    results = [jnp.zeros((rows, PAIRS), jnp.float32) for _ in range(planes)]
-    for lane in range(lanes):
-        for plane in range(planes):
-            piece = arrived_ref[lane, plane * rows : (plane + 1) * rows, :]
-            energy = plane * lanes + lane
-            for target in range(planes):
-                results[target] = results[target] + weights[target][energy : energy + 1, :] * piece
-    for plane in range(planes):
+            total = total + arrived_ref[plane * members + member]
+        totals.append(total)
+    own = lanes_of() // SHARE
+    for lane in range(LANES):
+        begin = lane * PAIRS
+        shared = jnp.zeros((1, PAIRS), jnp.float32)
+        for plane in range(PLANES):
+            tail = jnp.where(own == lane, totals[plane][:, LANES * PAIRS :], 0.0)
+            shared = shared + pltpu.roll(tail, (SHARE * (plane - lane)) % PAIRS, 1)
+        for column in range(out_ref.shape[0] // LANES):
+            piece = column * LANES + lane
+            for plane in range(PLANES):
+                out_ref[piece, :, plane * PAIRS : (plane + 1) * PAIRS] = totals[plane][
+                    :, begin : begin + PAIRS
+                ]
+            out_ref[piece, :, PLANES * PAIRS :] = shared
+
+
+def convolve_kernel(
+    lane_ref, shift_ref, occupation_ref, coupling_ref, arrived_ref, out_ref, sums_ref, tails_ref
+):
+    energies = PLANES * LANES
+    for lane in range(LANES):
+        total = arrived_ref[lane]
+        for column in range(1, arrived_ref.shape[0] // LANES):
+            total = total + arrived_ref[column * LANES + lane]
+        for plane in range(PLANES):
+            energy = plane * LANES + lane
+            sums_ref[energy : energy + 1, :PAIRS] = total[:, plane * PAIRS : (plane + 1) * PAIRS]
+        tails_ref[lane : lane + 1, :] = total[:, PLANES * PAIRS :]
+    kept = lanes_of() < SHARE
+    tails = tails_ref[...]
+    for plane in range(PLANES):
+        moved = pltpu.roll(tails, (-SHARE * plane) % PAIRS, 1)
+        sums_ref[plane * LANES : (plane + 1) * LANES, PAIRS:] = jnp.where(kept, moved, 0.0)
+    target = lax.broadcasted_iota(jnp.int32, (energies, energies), 0)
+    source = lax.broadcasted_iota(jnp.int32, (energies, energies), 1)
+    factors = []
+    for mode in range(MODES):
+        occupied = occupation_ref[mode] / MOMENTA
+        more = (occupation_ref[mode] + 1.0) / MOMENTA
+        shift = shift_ref[mode]
+        factors.append(
+            jnp.where(source == target - shift, occupied, 0.0)
+            + jnp.where(source == target + shift, more, 0.0)
+        )
+    shifted = lax.dot_general(
+        jnp.concatenate(factors, axis=0),
+        sums_ref[...],
+        (((1,), (0,)), ((), ())),
+        precision=lax.Precision.HIGHEST,
+        preferred_element_type=jnp.float32,
+    )
+    coupling = coupling_ref[...]
+    own_coupling = pltpu.roll(coupling, (PAIRS - SHARE * lane_ref[0]) % PAIRS, 1)
+    both = jnp.concatenate([coupling, own_coupling], axis=1)
+    result = jnp.zeros((energies, 2 * PAIRS), jnp.float32)
+    for mode in range(MODES):
+        result = result + shifted[mode * energies : (mode + 1) * energies] * both[mode : mode + 1]
+    tails = jnp.zeros((LANES, PAIRS), jnp.float32)
+    for plane in range(PLANES):
+        piece = jnp.where(kept, result[plane * LANES : (plane + 1) * LANES, PAIRS:], 0.0)
+        tails = tails + pltpu.roll(piece, SHARE * plane, 1)
+    for lane in range(LANES):
+        for plane in range(PLANES):
+            energy = plane * LANES + lane
+            out_ref[lane, :, plane * PAIRS : (plane + 1) * PAIRS] = result[
+                energy : energy + 1, :PAIRS
+            ]
+        out_ref[lane, :, PLANES * PAIRS :] = tails[lane : lane + 1]
+
+
+def spread_kernel(arrived_ref, out_ref):
+    copies = out_ref.shape[0] // PLANES
+    own = lanes_of() // SHARE
+    for plane in range(PLANES):
+        pieces = []
+        shared = jnp.zeros((1, PAIRS), jnp.float32)
+        for lane in range(LANES):
+            pieces.append(arrived_ref[lane, :, plane * PAIRS : (plane + 1) * PAIRS])
+            tail = jnp.where(own == plane, arrived_ref[lane, :, PLANES * PAIRS :], 0.0)
+            shared = shared + pltpu.roll(tail, (SHARE * (lane - plane)) % PAIRS, 1)
+        whole = jnp.concatenate(pieces + [shared], axis=1)
         for copy in range(copies):
-            out_ref[plane * copies + copy] = results[plane]
+            out_ref[plane * copies + copy] = whole
+
+
+def kernel_call(kernel, name, shape, *arguments, scalars=0, scratch=()):
+    return pl.pallas_call(
+        kernel,
+        out_shape=jax.ShapeDtypeStruct(shape, jnp.float32),
+        in_specs=[pl.BlockSpec(memory_space=pltpu.SMEM)] * scalars
+        + vmem(len(arguments) - scalars),
+        out_specs=vmem(1)[0],
+        scratch_shapes=[pltpu.VMEM(extent, jnp.float32) for extent in scratch],
+        name=name,
+        interpret=INTERPRET,
+    )(*arguments)
 
 
 def per_device(
@@ -304,44 +380,38 @@
     occupation,
     phonon_coupling,
 ):
-    planes = lax.axis_size("y")
-    lanes = lax.axis_size("z_lo")
-    slab = planes * lax.axis_size("x") * lax.axis_size("core")
-    rows = ROWS // slab
+    slab = PLANES * lax.axis_size("x") * lax.axis_size("core")
+    width = PLANES * PAIRS + PAIRS
     energy_index = lax.axis_index(("y", "z_lo"))
-    energy = -1.0 + 2.0 * (energy_index.astype(jnp.float32) + 0.5) / (planes * lanes)
+    energy = -1.0 + 2.0 * (energy_index.astype(jnp.float32) + 0.5) / (PLANES * LANES)
     system, green, blocks = first_call(
         energy[None], device_hamiltonian, lead_hamiltonian, lead_coupling, pair_atoms, slab
     )
     arrived = exchange(blocks, ("y", "x", "core"))
-    summed = pl.pallas_call(
-        slab_sum_kernel,
-        out_shape=jax.ShapeDtypeStruct((planes * rows, PAIRS), jnp.float32),
-        in_specs=vmem(1),
-        out_specs=vmem(1)[0],
-        name="slab_sum",
-        interpret=INTERPRET,
-    )(arrived)
-    near = lax.ppermute(summed, "z_hi", [(0, 1), (1, 0), (2, 3), (3, 2)])
-    paired = summed + near
-    far = lax.ppermute(paired, "z_hi", [(0, 3), (3, 0), (1, 2), (2, 1)])
-    copies = jnp.broadcast_to(paired + far, (lanes, planes * rows, PAIRS))
-    arrived = exchange(copies, "z_lo")
-    self_energy = pl.pallas_call(
+    columns = lax.axis_size("z_hi")
+    summed = kernel_call(slab_sum_kernel, "slab_sum", (columns * LANES, 1, width), arrived)
+    arrived = exchange(summed, ("z_hi", "z_lo"))
+    shifted = kernel_call(
         convolve_kernel,
-        out_shape=jax.ShapeDtypeStruct((slab, rows, PAIRS), jnp.float32),
-        in_specs=[pl.BlockSpec(memory_space=pltpu.SMEM)] * 3 + vmem(2),
-        out_specs=vmem(1)[0],
-        name="phonon_sum",
-        interpret=INTERPRET,
-    )(lax.axis_index("z_lo")[None], phonon_shift, occupation, phonon_coupling, arrived)
-    arrived = exchange(self_energy, ("y", "x", "core"))
+        "phonon_sum",
+        (LANES, 1, width),
+        lax.axis_index("z_lo")[None],
+        phonon_shift,
+        occupation,
+        phonon_coupling,
+        arrived,
+        scalars=3,
+        scratch=((PLANES * LANES, 2 * PAIRS), (LANES, PAIRS)),
+    )
+    arrived = exchange(shifted, "z_lo")
+    spread = kernel_call(spread_kernel, "spread", blocks.shape, arrived)
+    arrived = exchange(spread, ("y", "x", "core"))
     return last_call(system, green, arrived, pair_atoms)
 
 
 def solution(mesh):
     momentum = ("x", "z_hi", "core")
-    split_mesh = Mesh(mesh.devices.reshape(4, 8, 4, 4, 2), ("y", "z_lo") + momentum)
+    split_mesh = Mesh(mesh.devices.reshape(PLANES, LANES, 4, 4, 2), ("y", "z_lo") + momentum)
     return jax.shard_map(
         per_device,
         mesh=split_mesh,

time: 105 us -> 119 us (1.13)
  blocking collectives: 59.6 us -> 99.8 us
  starting transfers between devices: 18.6 us -> 0 us
  waiting for transfers between devices: 8.92 us -> 0 us
  Pallas kernels: 16.8 us -> 18.4 us
    all_to_all x3 -> x4, blocking collectives: 59.6 us -> 99.8 us  [exchange(): return lax.all_to_all(array, axes, split_axis=0, concat_axis=0, tiled=True)]
    ppermute x2 -> x0, starting transfers between devices: 18.6 us -> none  [the longest x1 12.9 us: per_device(): far = lax.ppermute(paired, 'z_hi', [(0, 3), (3, 0), (1, 2), (2, 1)])]
    ppermute x2 -> x0, waiting for transfers between devices: 8.92 us -> none  [the longest x1 7.76 us: per_device(): near = lax.ppermute(summed, 'z_hi', [(0, 1), (1, 0), (2, 3), (3, 2)])]
    pallas_call x2 -> x3, Pallas kernels: 3.41 us -> 5.08 us  [kernel_call(): pl.pallas_call(kernel, out_shape=jax.ShapeDtypeStruct(shape, jnp.float32)...]
  transfers between devices with their start and end apart: 2 -> 0, of which waited for: 2 -> 0; matrix products, arithmetic and copies ran while one was open for 0% -> 0% of each run, Pallas kernels for 0% -> 0%
where the time goes in v2:
time: 119 us; the launch traced here: 118 us
  blocking collectives  99.8 us (84%)
  Pallas kernels  18.4 us (15%)
    all_to_all x4, blocking collectives, exchange(): return lax.all_to_all(array, axes, split_axis=0, concat_axis=0, tiled=True)  99.8 us
    pallas_call x1, Pallas kernels, first_call(): pl.pallas_call(first_kernel, out_shape=(shape, shape, blocks), in_specs=[...  8.29 us
    pallas_call x3, Pallas kernels, kernel_call(): pl.pallas_call(kernel, out_shape=jax.ShapeDtypeStruct(shape, jnp.float32)...  5.08 us
    pallas_call x1, Pallas kernels, last_call(): pl.pallas_call(last_kernel, out_shape=jax.ShapeDtypeStruct((1, 1, 2, B, B...  5.05 us

profile of v2, /device:TPU:1, one launch (start us, length us, event | category | flops | bytes accessed | tf_op | source)
XLA Modules:
  0.0 118.2 jit_solution(10975573614371293208)
XLA Ops:
  0.0 8.3 %first_round.1 = (f32[2,256,256]{2,1,0:T(8,128)}, f32[2,256,256]{2,1,0:T(8,128)}, f32[32,1,1152]{2,1,0:T(1,128)}) custom-call(f32[1]{0:T(128)} %bitcast.energy_ref, f32[1,2,256,256]{3,2,1,0:T(8,128)} %device_ref.1, f32[1,2,256,256]{3,2,1,0:T(8,128)} %lead_ref.1, f32[1,2,256,256]{3,2,1,0:T(8,128)} %coupling_ref.2, s32[2,128]{1,0:T(2,128)} %pair_ref.3), custom_call_target="tpu_custom_call" | custom-call | tf_op jit(solution)/shard_map/first_round/pallas_call | solution.py:237
  8.3 26.2 %all_to_all.20.arrived_ref = f32[32,1,1152]{2,1,0:T(1,128)} all-to-all(f32[32,1,1152]{2,1,0:T(1,128)} %get-tuple-element.10), channel_id=1, replica_groups=mesh['y'=4,'z_lo'=8,'x'=4,'z_hi'=4,'core'=2] {'y','x','core'}, dimensions={0} | all-to-all | bytes 294912 | tf_op jit(solution)/shard_map/all_to_all | solution.py:261
  34.5 1.7 %slab_sum.1 = f32[32,1,640]{2,1,0:T(1,128)} custom-call(f32[32,1,1152]{2,1,0:T(1,128)} %all_to_all.20.arrived_ref), custom_call_target="tpu_custom_call" | custom-call | tf_op jit(solution)/shard_map/slab_sum/pallas_call | solution.py:362
  36.1 44.7 %all_to_all.21.arrived_ref = f32[32,1,640]{2,1,0:T(1,128)} all-to-all(f32[32,1,640]{2,1,0:T(1,128)} %slab_sum.1), channel_id=1, replica_groups=mesh['y'=4,'z_lo'=8,'x'=4,'z_hi'=4,'core'=2] {'z_hi','z_lo'}, dimensions={0} | all-to-all | bytes 163840 | tf_op jit(solution)/shard_map/all_to_all | solution.py:261
  80.8 1.9 %phonon_sum.1 = f32[8,1,640]{2,1,0:T(1,128)} custom-call(s32[1]{0:T(128)} %bitcast.1.lane_ref, s32[4]{0:T(128)} %shift_ref.1, f32[4]{0:T(128)} %occupation_ref.1, f32[4,128]{1,0:T(4,128)} %coupling_ref.3, f32[32,1,640]{2,1,0:T(1,128)} %all_to_all.21.arrived_ref), custom_call_target="tpu_custom_call" | custom-call | tf_op jit(solution)/shard_map/phonon_sum/pallas_call | solution.py:362
  82.7 13.3 %all_to_all.22.arrived_ref = f32[8,1,640]{2,1,0:T(1,128)} all-to-all(f32[8,1,640]{2,1,0:T(1,128)} %phonon_sum.1), channel_id=1, replica_groups=mesh['y'=4,'z_lo'=8,'x'=4,'z_hi'=4,'core'=2] {'z_lo'}, dimensions={0} | all-to-all | bytes 40960 | tf_op jit(solution)/shard_map/all_to_all | solution.py:261
  96.0 1.5 %spread.1 = f32[32,1,1152]{2,1,0:T(1,128)} custom-call(f32[8,1,640]{2,1,0:T(1,128)} %all_to_all.22.arrived_ref), custom_call_target="tpu_custom_call" | custom-call | tf_op jit(solution)/shard_map/spread/pallas_call | solution.py:362
  97.5 15.6 %all_to_all.23.blocks_ref = f32[32,1,1152]{2,1,0:T(1,128)} all-to-all(f32[32,1,1152]{2,1,0:T(1,128)} %spread.1), channel_id=1, replica_groups=mesh['y'=4,'z_lo'=8,'x'=4,'z_hi'=4,'core'=2] {'y','x','core'}, dimensions={0} | all-to-all | bytes 294912 | tf_op jit(solution)/shard_map/all_to_all | solution.py:261
  113.1 5.0 %second_round.1 = f32[1,1,2,256,256]{4,3,2,1,0:T(8,128)} custom-call(f32[2,256,256]{2,1,0:T(8,128)} %get-tuple-element.8.system_ref, f32[2,256,256]{2,1,0:T(8,128)} %get-tuple-element.9.green_ref, f32[32,1,1152]{2,1,0:T(1,128)} %all_to_all.23.blocks_ref, s32[2,128]{1,0:T(2,128)} %pair_ref.3), custom_call_target="tpu_custom_call" | custom-call | tf_op jit(solution)/shard_map/second_round/pallas_call | solution.py:249

commit v3 on v1

--- a/solution.py
+++ b/solution.py
@@ -12,6 +12,8 @@
 PAIRS = 128
 MODES = 4
 MOMENTA = 32
+PLANES = 4
+LANES = 8
 ROWS = 2 * ORB * ORB
 HALVES = (ATOMS + 1) // 2
 
@@ -75,7 +77,7 @@
     return lax.broadcasted_iota(jnp.int32, shape, axis)
 
 
-def inverse_of(system, bare):
+def error_and_start(system, bare):
     system_real, system_imag = system
     bare_real, bare_imag = bare
     identity = (grid_of(0) == grid_of(1)).astype(jnp.float32)
@@ -93,7 +95,12 @@
         plus_real * row_real - error_imag * row_imag,
         plus_real * row_imag + error_imag * row_real,
     )
-    error_parts = split_complex(error_real, error_imag)
+    return (error_real, error_imag), start
+
+
+def inverse_of(system, bare):
+    error, start = error_and_start(system, bare)
+    error_parts = split_complex(*error)
     squared = times(left_factors(error_parts), error_parts)
     return two_more(squared, start)
 
@@ -107,17 +114,47 @@
     return add(first, times(fourth_left, split_complex(*first)))
 
 
+def contact_of(system, coupling):
+    error, start = error_and_start(system, system)
+    error_parts = split_complex(*error)
+    coupling_parts = split_complex(*coupling)
+    right = times(left_factors(split_complex(*start)), coupling_parts, transposed=True)
+    squared_parts = split_complex(*times(left_factors(error_parts), error_parts))
+    fourth = times(left_factors(squared_parts), squared_parts)
+    left = add(coupling, times(left_factors(coupling_parts), squared_parts))
+    left = add(left, times(left_factors(split_complex(*left)), split_complex(*fourth)))
+    return times(left_factors(split_complex(*left)), split_complex(*right))
+
+
 def first_kernel(
-    energy_ref, device_ref, lead_ref, coupling_ref, pair_ref, system_ref, green_ref, blocks_ref, rows_ref
+    energy_ref,
+    device_hbm,
+    lead_hbm,
+    coupling_hbm,
+    pair_ref,
+    system_ref,
+    green_ref,
+    blocks_ref,
+    rows_ref,
+    device_ref,
+    lead_ref,
+    coupling_ref,
+    semaphores,
 ):
+    lead_copy = pltpu.make_async_copy(lead_hbm.at[0], lead_ref, semaphores.at[0])
+    coupling_copy = pltpu.make_async_copy(coupling_hbm.at[0], coupling_ref, semaphores.at[1])
+    device_copy = pltpu.make_async_copy(device_hbm.at[0], device_ref, semaphores.at[2])
+    lead_copy.start()
+    coupling_copy.start()
+    device_copy.start()
     energy = energy_ref[0]
     scaled_identity = jnp.where(grid_of(0) == grid_of(1), energy, 0.0)
-    lead = (scaled_identity - lead_ref[0, 0], -lead_ref[0, 1])
-    green_lead = inverse_of(lead, lead)
-    coupling_parts = split_complex(coupling_ref[0, 0], coupling_ref[0, 1])
-    half = times(left_factors(coupling_parts), split_complex(*green_lead))
-    contact = times(left_factors(split_complex(*half)), coupling_parts, transposed=True)
-    bare = (scaled_identity - device_ref[0, 0], -device_ref[0, 1])
+    lead_copy.wait()
+    coupling_copy.wait()
+    lead = (scaled_identity - lead_ref[0], -lead_ref[1])
+    contact = contact_of(lead, (coupling_ref[0], coupling_ref[1]))
+    device_copy.wait()
+    bare = (scaled_identity - device_ref[0], -device_ref[1])
     system = (bare[0] - contact[0], bare[1] - contact[1])
     system_ref[0] = system[0]
     system_ref[1] = system[1]
@@ -125,9 +162,11 @@
     green_ref[0] = green[0]
     green_ref[1] = green[1]
     take_blocks(green, pair_ref, rows_ref)
-    shards, shard_rows = blocks_ref.shape[:2]
-    for shard in range(shards):
-        blocks_ref[shard] = rows_ref[shard * shard_rows : (shard + 1) * shard_rows, :]
+    shards = blocks_ref.shape[0]
+    shard_rows = ROWS // shards
+    for row in range(ROWS):
+        place = (row % shard_rows) * PAIRS
+        blocks_ref[row // shard_rows, :, place : place + PAIRS] = rows_ref[row : row + 1, :]
 
 
 def take_blocks(green, pair_ref, rows_ref):
@@ -206,10 +245,12 @@
     return results
 
 
-def last_kernel(system_ref, green_ref, blocks_ref, pair_ref, out_ref):
-    shards, shard_rows = blocks_ref.shape[:2]
-    values = jnp.concatenate([blocks_ref[shard] for shard in range(shards)], axis=0)
-    scattering = place_blocks(values, pair_ref)
+def last_kernel(system_ref, green_ref, blocks_ref, pair_ref, out_ref, rows_ref):
+    shard_rows = ROWS // blocks_ref.shape[0]
+    for row in range(ROWS):
+        place = (row % shard_rows) * PAIRS
+        rows_ref[row : row + 1, :] = blocks_ref[row // shard_rows, :, place : place + PAIRS]
+    scattering = place_blocks(rows_ref, pair_ref)
     second = (system_ref[0] - scattering[0], system_ref[1] - scattering[1])
     green = (green_ref[0], green_ref[1])
     identity = (grid_of(0) == grid_of(1)).astype(jnp.float32)
@@ -224,15 +265,27 @@
     return [pl.BlockSpec(memory_space=pltpu.VMEM)] * count
 
 
+def near_core(array):
+    return array if INTERPRET else pltpu.with_memory_space_constraint(array, pltpu.VMEM)
+
+
+def near_shape(*shape):
+    return jax.ShapeDtypeStruct(shape, jnp.float32) if INTERPRET else pltpu.VMEM(shape, jnp.float32)
+
+
 def first_call(energy, device_hamiltonian, lead_hamiltonian, lead_coupling, pair_atoms, shards):
-    shape = jax.ShapeDtypeStruct((2, B, B), jnp.float32)
-    blocks = jax.ShapeDtypeStruct((shards, ROWS // shards, PAIRS), jnp.float32)
+    shape = near_shape(2, B, B)
+    blocks = near_shape(shards, 1, ROWS // shards * PAIRS)
     return pl.pallas_call(
         first_kernel,
         out_shape=(shape, shape, blocks),
-        in_specs=[pl.BlockSpec(memory_space=pltpu.SMEM)] + vmem(4),
+        in_specs=[pl.BlockSpec(memory_space=pltpu.SMEM)]
+        + [pl.BlockSpec(memory_space=pl.ANY)] * 3
+        + vmem(1),
         out_specs=tuple(vmem(3)),
-        scratch_shapes=[pltpu.VMEM((ROWS, PAIRS), jnp.float32)],
+        scratch_shapes=[pltpu.VMEM((ROWS, PAIRS), jnp.float32)]
+        + [pltpu.VMEM((2, B, B), jnp.float32)] * 3
+        + [pltpu.SemaphoreType.DMA((3,))],
         name="first_round",
         interpret=INTERPRET,
     )(energy, device_hamiltonian, lead_hamiltonian, lead_coupling, pair_atoms)
@@ -244,9 +297,10 @@
         out_shape=jax.ShapeDtypeStruct((1, 1, 2, B, B), jnp.float32),
         in_specs=vmem(4),
         out_specs=pl.BlockSpec(memory_space=pltpu.VMEM),
+        scratch_shapes=[pltpu.VMEM((ROWS, PAIRS), jnp.float32)],
         name="second_round",
         interpret=INTERPRET,
-    )(system, green, blocks, pair_atoms)
+    )(near_core(system), near_core(green), near_core(blocks), pair_atoms)
 
 
 def exchange(array, axes):
@@ -254,20 +308,31 @@
 
 
 def slab_sum_kernel(arrived_ref, out_ref):
-    rows = arrived_ref.shape[1]
-    groups = out_ref.shape[0] // rows
-    members = arrived_ref.shape[0] // groups
-    for group in range(groups):
-        total = arrived_ref[group * members]
+    members = arrived_ref.shape[0] // PLANES
+    rows = out_ref.shape[0] // PLANES
+    for plane in range(PLANES):
+        total = arrived_ref[plane * members]
         for member in range(1, members):
-            total = total + arrived_ref[group * members + member]
-        out_ref[group * rows : (group + 1) * rows, :] = total
+            total = total + arrived_ref[plane * members + member]
+        for row in range(rows):
+            place = plane * rows + row
+            out_ref[place : place + 1, :] = total[:, row * PAIRS : (row + 1) * PAIRS]
+
+
+def pair_kernel(own_ref, arrived_ref, out_ref):
+    out_ref[...] = own_ref[...] + arrived_ref[...]
+
+
+def copies_kernel(own_ref, arrived_ref, out_ref):
+    total = own_ref[...] + arrived_ref[...]
+    for copy in range(out_ref.shape[0]):
+        out_ref[copy] = total
 
 
 def convolve_kernel(lane_ref, shift_ref, occupation_ref, coupling_ref, arrived_ref, out_ref):
     lanes, stacked = arrived_ref.shape[:2]
-    rows = out_ref.shape[1]
-    planes = stacked // rows
+    planes = PLANES
+    rows = stacked // planes
     copies = out_ref.shape[0] // planes
     energies = lanes * planes
     source = lax.broadcasted_iota(jnp.int32, (energies, PAIRS), 0)
@@ -291,8 +356,27 @@
             for target in range(planes):
                 results[target] = results[target] + weights[target][energy : energy + 1, :] * piece
     for plane in range(planes):
-        for copy in range(copies):
-            out_ref[plane * copies + copy] = results[plane]
+        for row in range(rows):
+            for copy in range(copies):
+                out_ref[plane * copies + copy, :, row * PAIRS : (row + 1) * PAIRS] = results[plane][
+                    row : row + 1
+                ]
+
+
+def kernel_call(kernel, name, shape, *arguments, scalars=0, scratch=()):
+    arguments = arguments[:scalars] + tuple(
+        near_core(argument) for argument in arguments[scalars:]
+    )
+    return pl.pallas_call(
+        kernel,
+        out_shape=near_shape(*shape),
+        in_specs=[pl.BlockSpec(memory_space=pltpu.SMEM)] * scalars
+        + vmem(len(arguments) - scalars),
+        out_specs=vmem(1)[0],
+        scratch_shapes=[pltpu.VMEM(extent, jnp.float32) for extent in scratch],
+        name=name,
+        interpret=INTERPRET,
+    )(*arguments)
 
 
 def per_device(
@@ -304,44 +388,38 @@
     occupation,
     phonon_coupling,
 ):
-    planes = lax.axis_size("y")
-    lanes = lax.axis_size("z_lo")
-    slab = planes * lax.axis_size("x") * lax.axis_size("core")
-    rows = ROWS // slab
+    slab = PLANES * lax.axis_size("x") * lax.axis_size("core")
     energy_index = lax.axis_index(("y", "z_lo"))
-    energy = -1.0 + 2.0 * (energy_index.astype(jnp.float32) + 0.5) / (planes * lanes)
+    energy = -1.0 + 2.0 * (energy_index.astype(jnp.float32) + 0.5) / (PLANES * LANES)
     system, green, blocks = first_call(
         energy[None], device_hamiltonian, lead_hamiltonian, lead_coupling, pair_atoms, slab
     )
     arrived = exchange(blocks, ("y", "x", "core"))
-    summed = pl.pallas_call(
-        slab_sum_kernel,
-        out_shape=jax.ShapeDtypeStruct((planes * rows, PAIRS), jnp.float32),
-        in_specs=vmem(1),
-        out_specs=vmem(1)[0],
-        name="slab_sum",
-        interpret=INTERPRET,
-    )(arrived)
+    rows = PLANES * ROWS // slab
+    summed = kernel_call(slab_sum_kernel, "slab_sum", (rows, PAIRS), arrived)
     near = lax.ppermute(summed, "z_hi", [(0, 1), (1, 0), (2, 3), (3, 2)])
-    paired = summed + near
+    paired = kernel_call(pair_kernel, "pair_sum", (rows, PAIRS), summed, near)
     far = lax.ppermute(paired, "z_hi", [(0, 3), (3, 0), (1, 2), (2, 1)])
-    copies = jnp.broadcast_to(paired + far, (lanes, planes * rows, PAIRS))
+    copies = kernel_call(copies_kernel, "column_sum", (LANES, rows, PAIRS), paired, far)
     arrived = exchange(copies, "z_lo")
-    self_energy = pl.pallas_call(
+    spread = kernel_call(
         convolve_kernel,
-        out_shape=jax.ShapeDtypeStruct((slab, rows, PAIRS), jnp.float32),
-        in_specs=[pl.BlockSpec(memory_space=pltpu.SMEM)] * 3 + vmem(2),
-        out_specs=vmem(1)[0],
-        name="phonon_sum",
-        interpret=INTERPRET,
-    )(lax.axis_index("z_lo")[None], phonon_shift, occupation, phonon_coupling, arrived)
-    arrived = exchange(self_energy, ("y", "x", "core"))
+        "phonon_sum",
+        blocks.shape,
+        lax.axis_index("z_lo")[None],
+        phonon_shift,
+        occupation,
+        phonon_coupling,
+        arrived,
+        scalars=3,
+    )
+    arrived = exchange(spread, ("y", "x", "core"))
     return last_call(system, green, arrived, pair_atoms)
 
 
 def solution(mesh):
     momentum = ("x", "z_hi", "core")
-    split_mesh = Mesh(mesh.devices.reshape(4, 8, 4, 4, 2), ("y", "z_lo") + momentum)
+    split_mesh = Mesh(mesh.devices.reshape(PLANES, LANES, 4, 4, 2), ("y", "z_lo") + momentum)
     return jax.shard_map(
         per_device,
         mesh=split_mesh,

time: 105 us -> 97.7 us (0.930)
  blocking collectives: 59.6 us -> 54.9 us
  Pallas kernels: 16.8 us -> 13.7 us
  starting transfers between devices: 18.6 us -> 21.3 us
  waiting for transfers between devices: 8.92 us -> 7.44 us
    all_to_all x3, blocking collectives: 59.6 us -> 54.9 us  [exchange(): return lax.all_to_all(array, axes, split_axis=0, concat_axis=0, tiled=True)]
    pallas_call x2 -> x4, Pallas kernels: 3.41 us -> 0.95 us  [kernel_call(): pl.pallas_call(kernel, out_shape=near_shape(*shape), in_specs=[pl.BlockSp...]
    ppermute x1, waiting for transfers between devices: 7.76 us -> 6.28 us  [per_device(): near = lax.ppermute(summed, 'z_hi', [(0, 1), (1, 0), (2, 3), (3, 2)])]
    ppermute x1, starting transfers between devices: 12.9 us -> 14.3 us  [per_device(): far = lax.ppermute(paired, 'z_hi', [(0, 3), (3, 0), (1, 2), (2, 1)])]
    ppermute x1, starting transfers between devices: 5.67 us -> 6.95 us  [per_device(): near = lax.ppermute(summed, 'z_hi', [(0, 1), (1, 0), (2, 3), (3, 2)])]
where the time goes in v3:
time: 97.7 us; the launch traced here: 97.4 us
  blocking collectives  54.9 us (56%)
  starting transfers between devices  21.3 us (22%)
  Pallas kernels  13.7 us (14%)
  waiting for transfers between devices  7.44 us (8%)
    all_to_all x3, blocking collectives, exchange(): return lax.all_to_all(array, axes, split_axis=0, concat_axis=0, tiled=True)  54.9 us
    ppermute x1, starting transfers between devices, per_device(): far = lax.ppermute(paired, 'z_hi', [(0, 3), (3, 0), (1, 2), (2, 1)])  14.3 us
    pallas_call x1, Pallas kernels, first_call(): pl.pallas_call(first_kernel, out_shape=(shape, shape, blocks), in_specs=[...  8.23 us
    ppermute x1, starting transfers between devices, per_device(): near = lax.ppermute(summed, 'z_hi', [(0, 1), (1, 0), (2, 3), (3, 2)])  6.95 us
    ppermute x1, waiting for transfers between devices, per_device(): near = lax.ppermute(summed, 'z_hi', [(0, 1), (1, 0), (2, 3), (3, 2)])  6.28 us
    pallas_call x1, Pallas kernels, last_call(): pl.pallas_call(last_kernel, out_shape=jax.ShapeDtypeStruct((1, 1, 2, B, B...  4.54 us
  transfers between devices with their start and end apart: 2, of which 2 were waited for; matrix products, arithmetic and copies ran while one was open for 0% of the time, Pallas kernels for 0%

profile of v3, /device:TPU:1, one launch (start us, length us, event | category | flops | bytes accessed | tf_op | source)
XLA Modules:
  0.0 97.4 jit_solution(10127649866850424695)
XLA Ops:
  0.0 8.2 %first_round.1 = (f32[2,256,256]{2,1,0:T(8,128)S(1)}, f32[2,256,256]{2,1,0:T(8,128)S(1)}, f32[32,1,1152]{2,1,0:T(1,128)S(1)}) custom-call(f32[1]{0:T(128)} %bitcast.energy_ref, f32[1,2,256,256]{3,2,1,0:T(8,128)} %device_hbm.1, f32[1,2,256,256]{3,2,1,0:T(8,128)} %lead_hbm.1, f32[1,2,256,256]{3,2,1,0:T(8,128)} %coupling_hbm.1, s32[2,128]{1,0:T(2,128)} %pair_ref.3), custom_call_target="tpu_custom_call" | custom-call | tf_op jit(solution)/shard_map/first_round/pallas_call | solution.py:279
  8.2 24.6 %all_to_all.15.arrived_ref = f32[32,1,1152]{2,1,0:T(1,128)S(1)} all-to-all(f32[32,1,1152]{2,1,0:T(1,128)S(1)} %get-tuple-element.10), channel_id=1, replica_groups=mesh['y'=4,'z_lo'=8,'x'=4,'z_hi'=4,'core'=2] {'y','x','core'}, dimensions={0} | all-to-all | bytes 294912 | tf_op jit(solution)/shard_map/all_to_all | solution.py:307
  32.9 6.9 %collective-permute-start = (f32[36,128]{1,0:T(8,128)S(1)}, f32[36,128]{1,0:T(8,128)S(1)}, u32[]{:S(2)}, u32[]{:S(2)}) collective-permute-start(f32[36,128]{1,0:T(8,128)S(1)} %slab_sum.1.own_ref), channel_id=1, source_target_pairs={{0,2},{2,0},{4,6},{6,4},{1,3},{3,1},{5,7},{7,5},{8,10},{10,8},{12,... | collective-permute-start | bytes 55304 | tf_op jit(solution)/shard_map/ppermute | solution.py:400
  39.8 6.3 %collective-permute-done.arrived_ref = f32[36,128]{1,0:T(8,128)S(1)} collective-permute-done((f32[36,128]{1,0:T(8,128)S(1)}, f32[36,128]{1,0:T(8,128)S(1)}, u32[]{:S(2)}, u32[]{:S(2)}) %collective-permute-start) | collective-permute-done | bytes 18464 | tf_op jit(solution)/shard_map/ppermute | solution.py:400
  46.1 14.3 %collective-permute-start.1 = (f32[36,128]{1,0:T(8,128)S(1)}, f32[36,128]{1,0:T(8,128)S(1)}, u32[]{:S(2)}, u32[]{:S(2)}) collective-permute-start(f32[36,128]{1,0:T(8,128)S(1)} %pair_sum.1.own_ref), channel_id=1, source_target_pairs={{0,6},{6,0},{2,4},{4,2},{1,7},{7,1},{3,5},{5,3},{8,14},{14,8},{10,... | collective-permute-start | bytes 55304 | tf_op jit(solution)/shard_map/ppermute | solution.py:402
  60.4 1.2 %collective-permute-done.1.arrived_ref = f32[36,128]{1,0:T(8,128)S(1)} collective-permute-done((f32[36,128]{1,0:T(8,128)S(1)}, f32[36,128]{1,0:T(8,128)S(1)}, u32[]{:S(2)}, u32[]{:S(2)}) %collective-permute-start.1) | collective-permute-done | bytes 18464 | tf_op jit(solution)/shard_map/ppermute | solution.py:402
  61.6 0.0 copy-start
  61.6 15.4 %all_to_all.16.arrived_ref = f32[8,36,128]{2,1,0:T(8,128)S(1)} all-to-all(f32[8,36,128]{2,1,0:T(8,128)S(1)} %column_sum.1), channel_id=1, replica_groups=mesh['y'=4,'z_lo'=8,'x'=4,'z_hi'=4,'core'=2] {'z_lo'}, dimensions={0} | all-to-all | bytes 294912 | tf_op jit(solution)/shard_map/all_to_all | solution.py:307
  77.1 0.0 copy-done
  77.1 0.9 phonon_sum.1
  78.0 14.9 %all_to_all.17.blocks_ref = f32[32,1,1152]{2,1,0:T(1,128)S(1)} all-to-all(f32[32,1,1152]{2,1,0:T(1,128)S(1)} %phonon_sum.1), channel_id=1, replica_groups=mesh['y'=4,'z_lo'=8,'x'=4,'z_hi'=4,'core'=2] {'y','x','core'}, dimensions={0} | all-to-all | bytes 294912 | tf_op jit(solution)/shard_map/all_to_all | solution.py:307
  92.8 4.5 %second_round.1 = f32[1,1,2,256,256]{4,3,2,1,0:T(8,128)} custom-call(f32[2,256,256]{2,1,0:T(8,128)S(1)} %get-tuple-element.8.system_ref, f32[2,256,256]{2,1,0:T(8,128)S(1)} %get-tuple-element.9.green_ref, f32[32,1,1152]{2,1,0:T(1,128)S(1)} %all_to_all.17.blocks_ref, s32[2,128]{1,0:T(2,128)} %pair_ref.3), custom_call_target="tpu_custom_call" | custom-call | tf_op jit(solution)/shard_map/second_round/pallas_call | solution.py:295
  (3 shorter events, 0.0 us)
Async XLA Ops:
  32.9 13.2 %collective-permute-start = (f32[36,128]{1,0:T(8,128)S(1)}, f32[36,128]{1,0:T(8,128)S(1)}, u32[]{:S(2)}, u32[]{:S(2)}) collective-permute-start(f32[36,128]{1,0:T(8,128)S(1)} %slab_sum.1.own_ref), channel_id=1, source_target_pairs={{0,2},{2,0},{4,6},{6,4},{1,3},{3,1},{5,7},{7,5},{8,10},{10,8},{12,... | collective-permute-start | bytes 55304 | tf_op jit(solution)/shard_map/ppermute | solution.py:400
  46.1 15.5 %collective-permute-start.1 = (f32[36,128]{1,0:T(8,128)S(1)}, f32[36,128]{1,0:T(8,128)S(1)}, u32[]{:S(2)}, u32[]{:S(2)}) collective-permute-start(f32[36,128]{1,0:T(8,128)S(1)} %pair_sum.1.own_ref), channel_id=1, source_target_pairs={{0,6},{6,0},{2,4},{4,2},{1,7},{7,1},{3,5},{5,3},{8,14},{14,8},{10,... | collective-permute-start | bytes 55304 | tf_op jit(solution)/shard_map/ppermute | solution.py:402
  61.6 15.4 %copy-start = (f32[4,128]{1,0:T(4,128)S(1)}, f32[4,128]{1,0:T(4,128)}, u32[]{:S(2)}) copy-start(f32[4,128]{1,0:T(4,128)} %coupling_ref.1) | copy-start | bytes 6148
